TPU v7x, 32 devices: a whole 2x2x4 slice. The times are simulated.
32 devices in a mesh: band: 4 (over y, x), dom: 8 (over z, core).
Axes of the slice: x: 2, y: 2, z: 4, core: 2. Of those that a mesh axis runs over, the one named last changes fastest.
Arguments:
- orbitals: float32 [1024, 32768], P('band', 'dom'), may hold values from -6 to 6
- projectors: float32 [256, 512, 128], P('dom'), may hold values from -0.25 to 0.25
- window_start: int32 [256], P('dom'), may hold values from 0 to 3584
- slot_atom: int32 [8, 32], replicated, may hold values from 0 to 23, as said below
- atom_home: int32 [24], replicated, may hold values from 0 to 23, as said below
- atom_matrices: float32 [24, 128, 128], P('dom'), may hold values from -0.1875 to 0.1875
- rotation: float32 [1024, 1024], P('band'), may hold values from -0.1875 to 0.1875
Outputs:
- rotated: float32 [1024, 32768], P('band', 'dom')
Inputs may be any that keep to these rules, and one draw needn't show every extreme that they name: `atom_home`: a permutation; atom a is owned by domain atom_home[a] // 3, so every domain owns 3 atoms. `slot_atom`: in one domain at most 8 windows have atoms of one owner; in every domain some owner has exactly 8 of them, and some owner has exactly 8 from every domain.
All inputs are finite; a program needn't handle non-finite values.
Results may differ from a plain program's by a relative error of at most 0.0003.
Values sent between devices are 32-bit elements; how exact they have to be, the bound alone decides.
No kernel may reach another device: no remote copies, remote signals or barrier semaphores. Data moves between devices by JAX's collectives and lax.ppermute only.
A program may use at most 128 MiB of HBM per device.

v0:
```python
import jax
import jax.numpy as jnp
from jax import lax
from jax.sharding import PartitionSpec as P

HIGHEST = lax.Precision.HIGHEST


def per_device(orbitals, projectors, window_start, slot_atom, atom_home, atom_matrices, rotation):
    own_domain = lax.axis_index("dom")
    slot_count = projectors.shape[0]
    window = projectors.shape[1]
    atom_count = atom_home.shape[0]
    columns = rotation
    base_field = jnp.dot(
        columns,
        lax.all_gather(orbitals, "band", axis=0, tiled=True),
        precision=HIGHEST,
        preferred_element_type=jnp.float32,
    )
    windows = jax.vmap(lambda offset: lax.dynamic_slice_in_dim(orbitals, offset, window, 1))(
        window_start
    )
    partials = jnp.einsum("sbw,swp->sbp", windows, projectors, precision=HIGHEST)
    atom_ids = jnp.arange(atom_count, dtype=jnp.int32)
    home_table = jnp.sum(
        jnp.where(slot_atom[:, :, None] == atom_ids[None, None, :], atom_home[None, None, :], 0),
        axis=2,
    )
    own_home = lax.dynamic_index_in_dim(home_table, own_domain, 0, keepdims=False)
    home_match = (atom_ids[:, None] == own_home[None, :]).astype(jnp.float32)
    per_atom = jnp.einsum("rs,sbp->rbp", home_match, partials, precision=HIGHEST)
    owned_sums = lax.psum_scatter(per_atom, "dom", scatter_dimension=0, tiled=True)
    owned_factors = jnp.einsum("abp,apq->abq", owned_sums, atom_matrices, precision=HIGHEST)
    columns = rotation
    owned_factors = jnp.einsum(
        "bc,scp->sbp",
        columns,
        lax.all_gather(owned_factors, "band", axis=1, tiled=True),
        precision=HIGHEST,
    )
    all_factors = lax.all_gather(owned_factors, "dom", axis=0, tiled=True)
    slot_factors = jnp.einsum("rs,rbp->sbp", home_match, all_factors, precision=HIGHEST)
    updates = jnp.einsum("sbq,swq->sbw", slot_factors, projectors, precision=HIGHEST)

    def add_window(slot_index, current):
        offset = window_start[slot_index]
        previous = lax.dynamic_slice_in_dim(current, offset, window, 1)
        return lax.dynamic_update_slice_in_dim(current, previous + updates[slot_index], offset, 1)

    corrected = lax.fori_loop(0, slot_count, add_window, base_field)
    return corrected


def solution(mesh):
    in_specs = (
        P("band", "dom"),
        P("dom", None, None),
        P("dom"),
        P(),
        P(),
        P("dom", None, None),
        P("band", None),
    )
    out_specs = P("band", "dom")
    return jax.shard_map(
        per_device, mesh=mesh, in_specs=in_specs, out_specs=out_specs, check_vma=False
    )
```

profile of v0, /device:TPU:0, one launch (start us, length us, event | category | flops | bytes accessed | tf_op | source)
XLA Modules:
  0.0 689.3 jit_solution(3986818245490201017)
XLA Ops:
  7.3 107.7 %while.15 = (s32[]{:T(128)}, f32[256,4096]{1,0:T(8,128)}, s32[32,2]{0,1:T(2,128)S(1)}, f32[32,256,512]{2,1,0:T(8,128)}, s32[]{:T(128)}) while((s32[]{:T(128)}, f32[256,4096]{1,0:T(8,128)}, s32[32,2]{0,1:T(2,128)S(1)}, f32[32,256,512]{2,1,0:T(8,128)}, s32[]{:T(128)}) %tuple.39), condition=%wide.while_cond, body=%wide.while_body.sunk | while | flops 2 | bytes 1049689 | solution.py:21
  115.1 19.3 %fusion.14 = f32[32,256,128]{2,1,0:T(8,128)S(1)} fusion(f32[32,256,512]{2,1,0:T(8,128)} %get-tuple-element.92, f32[32,512,128]{2,1,0:T(8,128)} %param.10), kind=kOutput, calls=%fused_computation.21 | convolution fusion | flops 6442450944 | bytes 29360128 | tf_op jit(solution)/shard_map/sbw,swp->sbp/dot_general | solution.py:24
  134.4 4.3 fusion.2
  141.0 43.3 %reduce-scatter.2.cloned.1.call-done = f32[3,256,128]{2,1,0:T(8,128)} async-done(((f32[24,256,128]{2,1,0:T(8,128)}), f32[3,256,128]{2,1,0:T(8,128)}) %reduce-scatter.2.cloned.1.call-update) | async-done | bytes 393232 | tf_op jit(solution)/shard_map/reduce_scatter | solution.py:33
  186.7 30.0 %all-gather.6.cloned.1.call-done = f32[3,1024,128]{2,1,0:T(8,128)} async-done(((f32[3,256,128]{2,1,0:T(8,128)}), f32[3,1024,128]{2,1,0:T(8,128)}) %all-gather.6.cloned.1.call-update) | async-done | bytes 1572880 | tf_op jit(solution)/shard_map/all_gather | solution.py:39
  216.7 4.0 convolution_bitcast_fusion
  222.3 37.8 %all-gather.8.cloned.1.call-done = f32[24,256,128]{2,1,0:T(8,128)} async-done(((f32[3,256,128]{2,1,0:T(8,128)}), f32[24,256,128]{2,1,0:T(8,128)}) %all-gather.8.cloned.1.call-update) | async-done | bytes 3145744 | tf_op jit(solution)/shard_map/all_gather | solution.py:42
  260.1 5.8 fusion.4
  265.9 21.7 %fusion = f32[32,256,512]{2,1,0:T(8,128)} fusion(f32[32,512,128]{2,1,0:T(8,128)} %param.10, f32[32,256,128]{2,0,1:T(8,128)S(1)} %fusion.4), kind=kOutput, calls=%fused_computation.3 | convolution fusion | flops 6442450944 | bytes 29360128 | tf_op jit(solution)/shard_map/sbq,swq->sbw/dot_general | solution.py:44
  287.6 130.4 %all-gather.4.cloned.1.call-done = f32[1024,4096]{1,0:T(8,128)} async-done(((f32[256,4096]{1,0:T(8,128)}), f32[1024,4096]{1,0:T(8,128)}) %all-gather.4.cloned.1.call-update) | async-done | bytes 16777232 | tf_op jit(solution)/shard_map/all_gather | solution.py:17
  418.0 18.0 %fusion.13 = f32[256,4096]{1,0:T(8,128)} fusion(f32[256,1024]{1,0:T(8,128)S(1)} %copy-done, f32[1024,4096]{1,0:T(8,128)} %all-gather.4.cloned.1.call-done), kind=kOutput, calls=%fused_computation.20 | convolution fusion | flops 12884901888 | bytes 22020096 | tf_op jit(solution)/shard_map/dot_general | solution.py:15
  436.0 246.8 %while.14 = (s32[]{:T(128)}, f32[256,4096]{1,0:T(8,128)}, s32[32]{0:T(128)S(1)}, f32[32,256,512]{2,1,0:T(8,128)}, s32[]{:T(128)}, /*index=5*/s32[]{:T(128)}, s32[]{:T(128)}) while((s32[]{:T(128)}, f32[256,4096]{1,0:T(8,128)}, s32[32]{0:T(128)S(1)}, f32[32,256,512]{2,1,0:T(8,128)}, s32[]{:T(128)}, /*index=5*/s32[]{:T(128)}, s32[]{:T(128)}) %tuple.53), condition=%wide.region_3.4_spmd, body=%wide.region_2.3_spmd.sunk | while | flops 131077 | bytes 2621575 | solution.py:51
  439.9 3.8 dynamic_update_slice.8
  447.6 3.8 dynamic_update_slice.8
  455.4 3.8 dynamic_update_slice.8
  463.1 3.8 dynamic_update_slice.8
  470.8 3.8 dynamic_update_slice.8
  478.5 3.8 dynamic_update_slice.8
  486.2 3.8 dynamic_update_slice.8
  509.2 3.8 dynamic_update_slice.8
  516.9 3.8 dynamic_update_slice.8
  524.6 3.8 dynamic_update_slice.8
  532.3 3.8 dynamic_update_slice.8
  540.1 3.8 dynamic_update_slice.8
  547.8 3.8 dynamic_update_slice.8
  555.5 3.8 dynamic_update_slice.8
  563.2 3.8 dynamic_update_slice.8
  570.9 3.8 dynamic_update_slice.8
  578.6 3.8 dynamic_update_slice.8
  586.4 3.8 dynamic_update_slice.8
  609.5 3.8 dynamic_update_slice.8
  617.2 3.8 dynamic_update_slice.8
  (198 shorter events, 226.6 us)
Async XLA Ops:
  6.5 210.2 %copy-start = (f32[256,1024]{1,0:T(8,128)S(1)}, f32[256,1024]{1,0:T(8,128)}, u32[]{:S(2)}) copy-start(f32[256,1024]{1,0:T(8,128)} %param.15) | copy-start | bytes 3145732
  6.5 108.5 %copy-start.2 = (s32[8,32]{1,0:T(8,128)S(1)}, s32[8,32]{1,0:T(8,128)}, u32[]{:S(2)}) copy-start(s32[8,32]{1,0:T(8,128)} %param.12) | copy-start | bytes 3076
  6.5 108.5 %copy-start.3 = (s32[24]{0:T(128)S(1)}, s32[24]{0:T(128)}, u32[]{:S(2)}) copy-start(s32[24]{0:T(128)} %param.13) | copy-start | bytes 292
  6.5 177.7 %reduce-scatter.2.cloned.1.call-start = ((), (), s32[]{:S(2)}) async-start(), calls=%async_computation.2 | async-start | bytes 3538944 | tf_op jit(solution)/shard_map/reduce_scatter | solution.py:33
  138.7 45.6 %copy-start.1 = (f32[3,128,128]{2,1,0:T(8,128)S(1)}, f32[3,128,128]{2,1,0:T(8,128)}, u32[]{:S(2)}) copy-start(f32[3,128,128]{2,1,0:T(8,128)} %param.14) | copy-start | bytes 589828
  140.9 75.8 %all-gather.6.cloned.1.call-start = ((), (), s32[]{:S(2)}) async-start(), calls=%async_computation.3 | async-start | bytes 1966080 | tf_op jit(solution)/shard_map/all_gather | solution.py:39
  186.5 73.6 %all-gather.8.cloned.1.call-start = ((), (), s32[]{:S(2)}) async-start(), calls=%async_computation.4 | async-start | bytes 3538944 | tf_op jit(solution)/shard_map/all_gather | solution.py:42
  221.7 196.3 %all-gather.4.cloned.1.call-start = ((), (), s32[]{:S(2)}) async-start(), calls=%async_computation.1 | async-start | bytes 20971520 | tf_op jit(solution)/shard_map/all_gather | solution.py:17
  287.6 148.4 %copy-start.4 = (s32[32]{0:T(128)S(1)}, s32[32]{0:T(128)}, u32[]{:S(2)}) copy-start(s32[32]{0:T(128)} %param.11) | copy-start | bytes 388
Sparse Core Ops, SparseCore 0:
  141.1 43.1 reduce-scatter.1
  186.6 30.0 all-gather.5
  221.8 38.2 all-gather.7
  261.8 156.1 all-gather.3
where the time goes:
time: 695 us; the launch traced here: 689 us
  local copies, waits for them, and re-layouts  251 us (36%)
  waiting for transfers between devices  242 us (35%)
  matrix products  75.2 us (11%)
  loops' own time  59.9 us (9%)
  other arithmetic  47.5 us (7%)
  between operations  13.2 us (2%)
    all_gather x1, waiting for transfers between devices, per_device(): lax.all_gather(orbitals, 'band', axis=0, tiled=True)  130 us
    dynamic_update_slice x32, local copies, waits for them, and re-layouts, add_window(): lax.dynamic_update_slice_in_dim(current, previous + updates[slot_index],...  120 us
    gather x96, local copies, waits for them, and re-layouts  108 us
    another operation x1, loops' own time, per_device(): corrected = lax.fori_loop(0, slot_count, add_window, base_field)  59.9 us
    add x32, other arithmetic, add_window(): previous + updates[slot_index]  46.6 us
    reduce_scatter x1, waiting for transfers between devices, per_device(): lax.psum_scatter(per_atom, 'dom', scatter_dimension=0, tiled=True)  43.3 us
    all_gather x1, waiting for transfers between devices, per_device(): all_factors = lax.all_gather(owned_factors, 'dom', axis=0, tiled=True)  37.8 us
    all_gather x1, waiting for transfers between devices, per_device(): lax.all_gather(owned_factors, 'band', axis=1, tiled=True)  30 us
  transfers between devices with their start and end apart: 4, of which 4 were waited for; matrix products, arithmetic and copies ran while one was open for 4% of the time, Pallas kernels for 0%

commit v1 on v0

--- a/solution.py
+++ b/solution.py
@@ -4,6 +4,18 @@
 from jax.sharding import PartitionSpec as P
 
 HIGHEST = lax.Precision.HIGHEST
+
+
+def collect(x, axis, dim):
+    ways, here = (lax.axis_size(axis), lax.axis_index(axis))
+    grown, reach = (x, 1)
+    while reach < ways:
+        theirs = lax.ppermute(grown, axis, [(d, d ^ reach) for d in range(ways)])
+        mine_first = jnp.concatenate([grown, theirs], axis=dim)
+        theirs_first = jnp.concatenate([theirs, grown], axis=dim)
+        grown = jnp.where(here & reach == 0, mine_first, theirs_first)
+        reach = 2 * reach
+    return grown
 
 
 def per_device(orbitals, projectors, window_start, slot_atom, atom_home, atom_matrices, rotation):
@@ -13,10 +25,7 @@
     atom_count = atom_home.shape[0]
     columns = rotation
     base_field = jnp.dot(
-        columns,
-        lax.all_gather(orbitals, "band", axis=0, tiled=True),
-        precision=HIGHEST,
-        preferred_element_type=jnp.float32,
+        columns, collect(orbitals, "band", 0), precision=HIGHEST, preferred_element_type=jnp.float32
     )
     windows = jax.vmap(lambda offset: lax.dynamic_slice_in_dim(orbitals, offset, window, 1))(
         window_start

time: 695 us -> 764 us (1.099)
  waiting for transfers between devices: 242 us -> 276 us
  matrix products: 75.2 us -> 89.4 us
  other arithmetic: 47.5 us -> 57.8 us
    ppermute x0 -> x2, waiting for transfers between devices: none -> 232 us  [collect(): theirs = lax.ppermute(grown, axis, [(d, d ^ reach) for d in range(ways)])]
    all_gather x1 -> x0, waiting for transfers between devices: 130 us -> none  [per_device(): lax.all_gather(orbitals, 'band', axis=0, tiled=True)]
    reduce_scatter x1, waiting for transfers between devices: 43.3 us -> 0.01 us  [per_device(): lax.psum_scatter(per_atom, 'dom', scatter_dimension=0, tiled=True)]
    all_gather x1, waiting for transfers between devices: 37.8 us -> 0.01 us  [per_device(): all_factors = lax.all_gather(owned_factors, 'dom', axis=0, tiled=True)]
    dot_general x1, matrix products: 18 us -> 32.9 us  [per_device(): jnp.dot(columns, collect(orbitals, 'band', 0), precision=HIGHEST, preferr...]
    all_gather x1, waiting for transfers between devices: 30 us -> 44.1 us  [per_device(): lax.all_gather(owned_factors, 'band', axis=1, tiled=True)]
    select_n x0 -> x1, other arithmetic: none -> 9.62 us  [collect(): grown = jnp.where(here & reach == 0, mine_first, theirs_first)]
  transfers between devices with their start and end apart: 4 -> 5, of which waited for: 4 -> 3; matrix products, arithmetic and copies ran while one was open for 4% -> 7% of each run, Pallas kernels for 0% -> 0%
where the time goes in v1:
time: 764 us; the launch traced here: 758 us
  waiting for transfers between devices  276 us (36%)
  local copies, waits for them, and re-layouts  255 us (33%)
  matrix products  89.4 us (12%)
  loops' own time  61.3 us (8%)
  other arithmetic  57.8 us (8%)
  between operations  13.2 us (2%)
    ppermute x2, waiting for transfers between devices, collect(): theirs = lax.ppermute(grown, axis, [(d, d ^ reach) for d in range(ways)])  232 us
    dynamic_update_slice x32, local copies, waits for them, and re-layouts, add_window(): lax.dynamic_update_slice_in_dim(current, previous + updates[slot_index],...  120 us
    gather x96, local copies, waits for them, and re-layouts  107 us
    another operation x1, loops' own time, per_device(): corrected = lax.fori_loop(0, slot_count, add_window, base_field)  61.3 us
    add x32, other arithmetic, add_window(): previous + updates[slot_index]  46.6 us
    all_gather x1, waiting for transfers between devices, per_device(): lax.all_gather(owned_factors, 'band', axis=1, tiled=True)  44.1 us
    dot_general x1, matrix products, per_device(): jnp.dot(columns, collect(orbitals, 'band', 0), precision=HIGHEST, preferr...  32.9 us
    dot_general x1, matrix products, per_device(): jnp.einsum('sbq,swq->sbw', slot_factors, projectors, precision=HIGHEST)  20.9 us
  transfers between devices with their start and end apart: 5, of which 3 were waited for; matrix products, arithmetic and copies ran while one was open for 7% of the time, Pallas kernels for 0%

profile of v1, /device:TPU:0, one launch (start us, length us, event | category | flops | bytes accessed | tf_op | source)
XLA Modules:
  0.0 758.2 jit_solution(10468257612858746101)
XLA Ops:
  7.3 107.1 %while.15 = (s32[]{:T(128)}, f32[256,4096]{1,0:T(8,128)}, s32[32,2]{0,1:T(2,128)S(1)}, f32[32,256,512]{2,1,0:T(8,128)}, s32[]{:T(128)}) while((s32[]{:T(128)}, f32[256,4096]{1,0:T(8,128)}, s32[32,2]{0,1:T(2,128)S(1)}, f32[32,256,512]{2,1,0:T(8,128)}, s32[]{:T(128)}) %tuple.43), condition=%wide.while_cond, body=%wide.while_body.sunk | while | flops 2 | bytes 1049689 | solution.py:30
  115.2 19.3 %fusion.22 = f32[32,256,128]{2,1,0:T(8,128)S(1)} fusion(f32[32,256,512]{2,1,0:T(8,128)} %get-tuple-element.92, f32[32,512,128]{2,1,0:T(8,128)} %param.10), kind=kOutput, calls=%fused_computation.31 | convolution fusion | flops 6442450944 | bytes 29360128 | tf_op jit(solution)/shard_map/sbw,swp->sbp/dot_general | solution.py:33
  134.5 4.3 fusion.10
  144.3 90.8 %collective-permute-done = f32[256,4096]{1,0:T(8,128)} collective-permute-done((f32[256,4096]{1,0:T(8,128)}, f32[256,4096]{1,0:T(8,128)}, u32[]{:S(2)}, u32[]{:S(2)}) %collective-permute-start) | collective-permute-done | bytes 4194336 | tf_op jit(solution)/shard_map/ppermute | solution.py:13
  235.1 9.6 %maximum_select_fusion.2 = f32[512,4096]{1,0:T(8,128)} fusion(f32[256,4096]{1,0:T(8,128)} %collective-permute-done, f32[256,4096]{1,0:T(8,128)} %get-tuple-element.216, pred[]{:T(512)S(6)} %eq.35), kind=kLoop, calls=%fused_computation.10 | loop fusion | flops 6291456 | bytes 16777216 | tf_op jit(solution)/shard_map/jit(_where)/select_n | solution.py:16
  248.8 44.1 %all-gather.3.cloned.1.call-done = f32[3,1024,128]{2,1,0:T(8,128)} async-done(((f32[3,256,128]{2,1,0:T(8,128)}), f32[3,1024,128]{2,1,0:T(8,128)}) %all-gather.3.cloned.1.call-update) | async-done | bytes 1572880 | tf_op jit(solution)/shard_map/all_gather | solution.py:48
  292.9 4.0 convolution_bitcast_fusion
  297.9 141.4 %collective-permute-done.1 = f32[512,4096]{1,0:T(8,128)} collective-permute-done((f32[512,4096]{1,0:T(8,128)}, f32[512,4096]{1,0:T(8,128)}, u32[]{:S(2)}, u32[]{:S(2)}) %collective-permute-start.1) | collective-permute-done | bytes 8388640 | tf_op jit(solution)/shard_map/ppermute | solution.py:13
  439.3 32.9 %fusion.7 = f32[256,4096]{0,1:T(8,128)} fusion(f32[256,1024]{1,0:T(8,128)S(1)} %copy-done, f32[512,4096]{1,0:T(8,128)} %collective-permute-done.1, f32[512,4096]{1,0:T(8,128)} %maximum_select_fusion.2, pred[]{:T(512)S(6)} %eq.34), kind=kOutput, calls=%fused_computation.12 | convolution fusion | flops 12897484800 | bytes 22020096 | tf_op jit(solution)/shard_map/dot_general | solution.py:27
  472.1 5.6 copy.23
  477.7 5.8 fusion.12
  483.6 20.9 %fusion.8 = f32[32,256,512]{2,1,0:T(8,128)} fusion(f32[32,512,128]{2,1,0:T(8,128)} %param.10, f32[32,256,128]{2,0,1:T(8,128)S(1)} %fusion.12), kind=kOutput, calls=%fused_computation.13 | convolution fusion | flops 6442450944 | bytes 29360128 | tf_op jit(solution)/shard_map/sbq,swq->sbw/dot_general | solution.py:53
  504.5 247.1 %while.14 = (s32[]{:T(128)}, f32[256,4096]{1,0:T(8,128)}, s32[32]{0:T(128)S(1)}, f32[32,256,512]{2,1,0:T(8,128)}, s32[]{:T(128)}, /*index=5*/s32[]{:T(128)}, s32[]{:T(128)}) while((s32[]{:T(128)}, f32[256,4096]{1,0:T(8,128)}, s32[32]{0:T(128)S(1)}, f32[32,256,512]{2,1,0:T(8,128)}, s32[]{:T(128)}, /*index=5*/s32[]{:T(128)}, s32[]{:T(128)}) %tuple.55), condition=%wide.region_3.4_spmd, body=%wide.region_2.3_spmd.sunk | while | flops 131077 | bytes 2621575 | solution.py:60
  508.5 3.8 dynamic_update_slice.8
  516.2 3.8 dynamic_update_slice.8
  523.9 3.8 dynamic_update_slice.8
  531.7 3.8 dynamic_update_slice.8
  539.4 3.8 dynamic_update_slice.8
  547.1 3.8 dynamic_update_slice.8
  554.8 3.8 dynamic_update_slice.8
  577.8 3.8 dynamic_update_slice.8
  585.6 3.8 dynamic_update_slice.8
  593.3 3.8 dynamic_update_slice.8
  601.0 3.8 dynamic_update_slice.8
  608.8 3.8 dynamic_update_slice.8
  616.5 3.8 dynamic_update_slice.8
  624.2 3.8 dynamic_update_slice.8
  631.9 3.8 dynamic_update_slice.8
  639.7 3.8 dynamic_update_slice.8
  678.3 3.8 dynamic_update_slice.8
  701.5 3.8 dynamic_update_slice.8
  740.2 3.8 dynamic_update_slice.8
  (199 shorter events, 233.6 us)
Async XLA Ops:
  6.5 286.4 %copy-start = (f32[256,1024]{1,0:T(8,128)S(1)}, f32[256,1024]{1,0:T(8,128)}, u32[]{:S(2)}) copy-start(f32[256,1024]{1,0:T(8,128)} %param.15) | copy-start | bytes 3145732
  6.5 240.0 %reduce-scatter.2.cloned.1.call-start = ((), (), s32[]{:S(2)}) async-start(), calls=%async_computation.1 | async-start | bytes 3538944 | tf_op jit(solution)/shard_map/reduce_scatter | solution.py:42
  141.0 151.9 %all-gather.3.cloned.1.call-start = ((), (), s32[]{:S(2)}) async-start(), calls=%async_computation.2 | async-start | bytes 1966080 | tf_op jit(solution)/shard_map/all_gather | solution.py:48
  141.2 93.9 %collective-permute-start = (f32[256,4096]{1,0:T(8,128)}, f32[256,4096]{1,0:T(8,128)}, u32[]{:S(2)}, u32[]{:S(2)}) collective-permute-start(f32[256,4096]{1,0:T(8,128)} %get-tuple-element.216), channel_id=1, source_target_pairs={{0,8},{8,0},{16,24},{24,16},{1,9},{9,1},{17,25},{25,17},{2,10},{10... | collective-permute-start | bytes 12582920 | tf_op jit(solution)/shard_map/ppermute | solution.py:13
  144.3 102.2 %copy-start.2 = (f32[3,128,128]{2,1,0:T(8,128)S(1)}, f32[3,128,128]{2,1,0:T(8,128)}, u32[]{:S(2)}) copy-start(f32[3,128,128]{2,1,0:T(8,128)} %param.14) | copy-start | bytes 589828
  244.7 194.5 %collective-permute-start.1 = (f32[512,4096]{1,0:T(8,128)}, f32[512,4096]{1,0:T(8,128)}, u32[]{:S(2)}, u32[]{:S(2)}) collective-permute-start(f32[512,4096]{1,0:T(8,128)} %maximum_select_fusion.2), channel_id=1, source_target_pairs={{0,16},{8,24},{16,0},{24,8},{1,17},{9,25},{17,1},{25,9},{2,18},{10... | collective-permute-start | bytes 25165832 | tf_op jit(solution)/shard_map/ppermute | solution.py:13
  248.8 229.0 %all-gather.5.cloned.1.call-start = ((), (), s32[]{:S(2)}) async-start(), calls=%async_computation.3 | async-start | bytes 3538944 | tf_op jit(solution)/shard_map/all_gather | solution.py:51
  483.6 20.9 %copy-start.3 = (s32[32]{0:T(128)S(1)}, s32[32]{0:T(128)}, u32[]{:S(2)}) copy-start(s32[32]{0:T(128)} %param.11) | copy-start | bytes 388
  483.6 268.0 %copy-start.1 = (f32[256,1024]{1,0:T(8,128)S(1)}, f32[256,1024]{1,0:T(8,128)}, u32[]{:S(2)}) copy-start(f32[256,1024]{1,0:T(8,128)} %param.15) | copy-start | bytes 3145732
Sparse Core Ops, SparseCore 0:
  141.1 43.0 reduce-scatter.1
  248.9 43.9 all-gather.2
  298.0 38.2 all-gather.4
